TPU v7x, 512 devices: a whole 4x4x16 slice. The times are simulated.
512 devices in a mesh: ctx: 16 (over y_lo, x, core), chan: 32 (over z, y_hi).
Axes of the slice: x: 4, y: 4 (y_hi: 2, y_lo: 2; y = y_hi * 2 + y_lo), z: 16, core: 2. Of those that a mesh axis runs over, the one named last changes fastest.
Arguments:
- query_stream: bfloat16 [16384, 4096], P('ctx', 'chan'), may hold values from -6 to 6
- key_stream: bfloat16 [16384, 4096], P('ctx', 'chan'), may hold values from -6 to 6
- value_stream: bfloat16 [16384, 4096], P('ctx', 'chan'), may hold values from -6 to 6
- short_weight: float32 [3, 7, 4096], P(None, None, 'chan'), may hold values from -2 to 2
- filter_rows: float32 [256, 16384], P(None, 'chan'), may hold values from -0.046875 to 0.046875
- skip_weight: float32 [4096], P('chan'), may hold values from -4 to 4
Outputs:
- gated: bfloat16 [16384, 4096], P('ctx', 'chan')
All inputs are finite; a program needn't handle non-finite values.
Results may differ from a plain program's by a relative error of at most 0.0064.
Values may be sent and summed in bfloat16 or wider, within the bound.
A program may use at most 64 MiB of HBM per device.

v0:
```python
import math

import jax
import jax.numpy as jnp
from jax import lax
from jax.sharding import PartitionSpec as P

GROUP = 16
KSHORT = 7


highest = lax.Precision.HIGHEST
high_pass = lax.Precision.HIGH


def widen(value):
    return lax.optimization_barrier(value).astype(jnp.float32)


def angle_table(count_rows, count_cols, period):
    indices = (
        lax.iota(jnp.int32, count_rows)[:, None] * lax.iota(jnp.int32, count_cols)[None, :] % period
    )
    angles = -2.0 * math.pi / period * indices.astype(jnp.float32)
    return (jnp.cos(angles), jnp.sin(angles))


def make_tables(half_rows, width_a):
    full_b = 2 * half_rows
    outer_cos, outer_sin = angle_table(full_b, full_b, full_b)
    twist_cos, twist_sin = angle_table(full_b, width_a, full_b * width_a)
    inner_cos, inner_sin = angle_table(width_a, width_a, width_a)
    return (outer_cos, outer_sin, twist_cos, twist_sin, inner_cos, inner_sin)


def forward_dft(signal, dft_tables, accuracy):
    outer_cos, outer_sin, twist_cos, twist_sin, inner_cos, inner_sin = dft_tables
    half_rows = signal.shape[1]
    first_re = jnp.einsum("kn,cna->cka", outer_cos[:, :half_rows], signal, precision=accuracy)
    first_im = jnp.einsum("kn,cna->cka", outer_sin[:, :half_rows], signal, precision=accuracy)
    turned_re = first_re * twist_cos - first_im * twist_sin
    turned_im = first_re * twist_sin + first_im * twist_cos
    spec_re = jnp.einsum("cka,aj->ckj", turned_re, inner_cos, precision=accuracy) - jnp.einsum(
        "cka,aj->ckj", turned_im, inner_sin, precision=accuracy
    )
    spec_im = jnp.einsum("cka,aj->ckj", turned_re, inner_sin, precision=accuracy) + jnp.einsum(
        "cka,aj->ckj", turned_im, inner_cos, precision=accuracy
    )
    return (spec_re, spec_im)


def inverse_dft(spec_re, spec_im, dft_tables, accuracy):
    outer_cos, outer_sin, twist_cos, twist_sin, inner_cos, inner_sin = dft_tables
    full_b = outer_cos.shape[0]
    half_rows = full_b // 2
    period = full_b * inner_cos.shape[0]
    back_re = jnp.einsum("ckj,ja->cka", spec_re, inner_cos, precision=accuracy) + jnp.einsum(
        "ckj,ja->cka", spec_im, inner_sin, precision=accuracy
    )
    back_im = jnp.einsum("ckj,ja->cka", spec_im, inner_cos, precision=accuracy) - jnp.einsum(
        "ckj,ja->cka", spec_re, inner_sin, precision=accuracy
    )
    plain_re = back_re * twist_cos + back_im * twist_sin
    plain_im = back_im * twist_cos - back_re * twist_sin
    signal = jnp.einsum(
        "nk,cka->cna", outer_cos[:half_rows], plain_re, precision=accuracy
    ) + jnp.einsum("nk,cka->cna", outer_sin[:half_rows], plain_im, precision=accuracy)
    return signal / period


def long_mix(columns, filt_re, filt_im, skip_local, dft_tables):
    channel_count, length = columns.shape
    block_count = filt_re.shape[0]
    per_block = channel_count // block_count

    def one_group(items):
        block_cols, block_skip, group_re, group_im = items
        signal = widen(block_cols)
        spec_re, spec_im = forward_dft(
            signal.reshape(per_block, length // 128, 128), dft_tables, high_pass
        )
        prod_re = spec_re * group_re - spec_im * group_im
        prod_im = spec_re * group_im + spec_im * group_re
        result = inverse_dft(prod_re, prod_im, dft_tables, high_pass).reshape(per_block, length)
        return (result + block_skip[:, None] * signal).astype(jnp.bfloat16)

    mixed = lax.map(
        one_group,
        (
            columns.reshape(block_count, per_block, length),
            skip_local.reshape(block_count, per_block),
            filt_re,
            filt_im,
        ),
    )
    return mixed.reshape(channel_count, length)


def causal_taps(extended, tap_weights, length, axis_index):
    rim_width = tap_weights.shape[0] - 1
    summed = tap_weights[0] * lax.slice_in_dim(
        extended, rim_width, rim_width + length, axis=axis_index
    )
    for offset in range(1, tap_weights.shape[0]):
        summed = summed + tap_weights[offset] * lax.slice_in_dim(
            extended, rim_width - offset, rim_width - offset + length, axis=axis_index
        )
    return summed


def local(query_stream, key_stream, value_stream, short_weight, filter_rows, skip_weight):
    pos_rows, width_dev = query_stream.shape
    ctx_size = lax.axis_size("ctx")
    chan_size = lax.axis_size("chan")
    ctx_place = lax.axis_index("ctx")
    chan_x = width_dev // ctx_size
    seq_len = pos_rows * ctx_size
    segment = filter_rows.shape[1]
    group_count = max(1, chan_x // GROUP)
    starts = lax.iota(jnp.int32, chan_size)[:, None] * width_dev + ctx_place * chan_x
    wanted = starts // GROUP + lax.iota(jnp.int32, group_count)[None, :]
    picked = jnp.take(filter_rows, wanted.reshape(-1), axis=0).reshape(
        chan_size, group_count, segment
    )
    full_rows = lax.all_to_all(picked, "chan", split_axis=0, concat_axis=2, tiled=True).reshape(
        group_count, seq_len
    )
    dft_tables = make_tables(seq_len // 128, 128)
    filt_re, filt_im = forward_dft(
        full_rows.reshape(group_count, seq_len // 128, 128), dft_tables, highest
    )
    skip_local = lax.dynamic_slice_in_dim(skip_weight, ctx_place * chan_x, chan_x, 0)
    moved = (
        lax.all_to_all(
            query_stream.reshape(pos_rows, ctx_size, chan_x),
            "ctx",
            split_axis=1,
            concat_axis=0,
            tiled=True,
        ),
        lax.all_to_all(
            key_stream.reshape(pos_rows, ctx_size, chan_x),
            "ctx",
            split_axis=1,
            concat_axis=0,
            tiled=True,
        ),
        lax.all_to_all(
            value_stream.reshape(pos_rows, ctx_size, chan_x),
            "ctx",
            split_axis=1,
            concat_axis=0,
            tiled=True,
        ),
    )
    local_taps = lax.dynamic_slice_in_dim(short_weight, ctx_place * chan_x, chan_x, 2)[
        :, :, :, None
    ]
    shorts = []
    for stream_index in range(3):
        columns = moved[stream_index].reshape(seq_len, chan_x).T.astype(jnp.float32)
        extended = jnp.pad(columns, ((0, 0), (KSHORT - 1, 0)))
        shorts.append(causal_taps(extended, local_taps[stream_index], seq_len, 1))
    q_short = shorts[0].astype(jnp.bfloat16)
    product = (shorts[1] * shorts[2]).astype(jnp.bfloat16)
    mixed = long_mix(product, filt_re, filt_im, skip_local, dft_tables)
    gated_cols = (widen(q_short) * widen(mixed)).astype(jnp.bfloat16)
    gated = lax.all_to_all(
        gated_cols.T.reshape(seq_len, 1, chan_x), "ctx", split_axis=0, concat_axis=1, tiled=True
    ).reshape(pos_rows, width_dev)
    return gated


def solution(mesh):
    return jax.shard_map(
        local,
        mesh=mesh,
        in_specs=(
            P("ctx", "chan"),
            P("ctx", "chan"),
            P("ctx", "chan"),
            P(None, None, "chan"),
            P(None, "chan"),
            P("chan"),
        ),
        out_specs=P("ctx", "chan"),
        check_vma=False,
    )
```

profile of v0, /device:TPU:1, one launch (start us, length us, event | category | flops | bytes accessed | tf_op | source)
XLA Modules:
  0.0 135.0 jit_solution(5902070258151117245)
XLA Ops:
  0.0 1.9 %copy.31 = bf16[1024,128]{0,1:T(8,128)(2,1)} copy(bf16[1024,128]{1,0:T(8,128)(2,1)} %param.7) | data formatting | bytes 524288 | tf_op args[1]
  1.9 10.2 %all-to-all-start.1 = ((bf16[1024,16,8]{0,2,1:T(8,128)(2,1)}), bf16[1024,16,8]{0,2,1:T(8,128)(2,1)S(1)}, u32[]{:S(2)}, u32[]{:S(2)}) async-start(bf16[1024,16,8]{0,2,1:T(8,128)(2,1)} %bitcast.16), calls=%async_computation.1 | async-start | bytes 524288 | tf_op jit(solution)/shard_map/all_to_all | solution.py:141
  14.6 1.8 %copy.32 = bf16[1024,128]{0,1:T(8,128)(2,1)} copy(bf16[1024,128]{1,0:T(8,128)(2,1)} %param.8) | data formatting | bytes 524288 | tf_op args[2]
  17.1 2.2 %all-to-all-done.1 = bf16[1024,16,8]{0,2,1:T(8,128)(2,1)S(1)} async-done(((bf16[1024,16,8]{0,2,1:T(8,128)(2,1)}), bf16[1024,16,8]{0,2,1:T(8,128)(2,1)S(1)}, u32[]{:S(2)}, u32[]{:S(2)}) %all-to-all-start.1) | async-done | bytes 262176 | tf_op jit(solution)/shard_map/all_to_all | solution.py:141
  19.3 4.1 %all-to-all-start.2 = ((bf16[1024,16,8]{0,2,1:T(8,128)(2,1)}), bf16[1024,16,8]{0,2,1:T(8,128)(2,1)S(1)}, u32[]{:S(2)}, u32[]{:S(2)}) async-start(bf16[1024,16,8]{0,2,1:T(8,128)(2,1)} %bitcast.31), calls=%async_computation.2 | async-start | bytes 524288 | tf_op jit(solution)/shard_map/all_to_all | solution.py:148
  25.9 1.8 %copy.30 = bf16[1024,128]{0,1:T(8,128)(2,1)} copy(bf16[1024,128]{1,0:T(8,128)(2,1)} %param.6) | data formatting | bytes 524288 | tf_op args[0]
  27.8 2.9 %all-to-all-done.2 = bf16[1024,16,8]{0,2,1:T(8,128)(2,1)S(1)} async-done(((bf16[1024,16,8]{0,2,1:T(8,128)(2,1)}), bf16[1024,16,8]{0,2,1:T(8,128)(2,1)S(1)}, u32[]{:S(2)}, u32[]{:S(2)}) %all-to-all-start.2) | async-done | bytes 262176 | tf_op jit(solution)/shard_map/all_to_all | solution.py:148
  30.7 4.1 %all-to-all-start = ((bf16[1024,16,8]{0,2,1:T(8,128)(2,1)}), bf16[1024,16,8]{0,2,1:T(8,128)(2,1)S(1)}, u32[]{:S(2)}, u32[]{:S(2)}) async-start(bf16[1024,16,8]{0,2,1:T(8,128)(2,1)} %bitcast.1), calls=%async_computation | async-start | bytes 524288 | tf_op jit(solution)/shard_map/all_to_all | solution.py:134
  34.9 1.7 %multiply_convert_fusion.1 = bf16[8,16384]{1,0:T(8,128)(2,1)S(1)} fusion(f32[8,16384]{1,0:T(8,128)S(1)} %bitcast.153, f32[8,16384]{1,0:T(8,128)S(1)} %bitcast.152, f32[8]{0:T(128)S(1)} %get-tuple-element.61, f32[8]{0:T(128)S(1)} %get-tuple-element.28, f32[8]{0:T(128)S(1)} %get-tuple-element.29, f32[8]{0:T(128)S(1)} %get-tuple-element.30, ...), kind=kLoop, calls=%fused_computation.32 | loop fusion | flops 3670016 | bytes 1311168 | tf_op jit(solution)/shard_map/convert_element_type | solution.py:165
  37.6 2.2 %fusion.25 = f32[8,256,128]{2,1,0:T(8,128)} fusion(f32[8,256,128]{1,2,0:T(8,128)S(1)} %convolution_bitcast_fusion, f32[8,256,128]{1,2,0:T(8,128)S(1)} %convolution_bitcast_fusion.1, f32[256,128]{0,1:T(8,128)S(1)} %get-tuple-element.62, f32[256,128]{0,1:T(8,128)S(1)} %get-tuple-element.63), kind=kOutput, calls=%fused_computation.51 | convolution fusion | flops 202342400 | bytes 3407872 | tf_op jit(solution)/shard_map/while/body/eval_jaxpr/cka,aj->ckj/dot_general | solution.py:46
  39.8 2.2 %fusion.26 = f32[8,256,128]{2,1,0:T(8,128)} fusion(f32[8,256,128]{1,2,0:T(8,128)S(1)} %convolution_bitcast_fusion, f32[8,256,128]{1,2,0:T(8,128)S(1)} %convolution_bitcast_fusion.1, f32[256,128]{0,1:T(8,128)S(1)} %get-tuple-element.62, f32[256,128]{0,1:T(8,128)S(1)} %get-tuple-element.63), kind=kOutput, calls=%fused_computation.52 | convolution fusion | flops 202342400 | bytes 3407872 | tf_op jit(solution)/shard_map/while/body/eval_jaxpr/cka,aj->ckj/dot_general | solution.py:43
  42.1 14.3 %all-to-all-start.3 = ((f32[32,1,512]{2,1,0:T(1,128)}), f32[32,1,512]{2,1,0:T(1,128)S(1)}, u32[]{:S(2)}, u32[]{:S(2)}) async-start(f32[32,1,512]{2,1,0:T(1,128)} %copy.37), calls=%async_computation.3 | async-start | bytes 131072 | tf_op jit(solution)/shard_map/all_to_all | solution.py:125
  56.4 1.6 %add_convert_fusion = bf16[8,16384]{1,0:T(8,128)(2,1)} fusion(f32[8,16384]{1,0:T(8,128)S(1)} %bitcast.154, f32[8]{0:T(128)S(1)} %get-tuple-element.55, f32[8]{0:T(128)S(1)} %get-tuple-element.56, f32[8]{0:T(128)S(1)} %get-tuple-element.57, f32[8]{0:T(128)S(1)} %get-tuple-element.58, f32[8]{0:T(128)S(1)} %get-tuple-element.59, f32[8]{0:T(128)S(1)} %get-tuple-element.60, ...), kind=kLoop, calls=%fused_computation.33 | loop fusion | flops 1835008 | bytes 786656 | tf_op jit(solution)/shard_map/convert_element_type | solution.py:164
  58.0 2.7 %convolution_add_fusion.1 = f32[8,256,128]{2,1,0:T(8,128)S(1)} fusion(f32[8,256,128]{2,1,0:T(8,128)} %fusion.25, f32[8,256,128]{1,2,0:T(8,128)S(1)} %convolution_bitcast_fusion, f32[8,256,128]{1,2,0:T(8,128)} %copy-done.2, f32[256,128]{0,1:T(8,128)S(1)} %get-tuple-element.62, f32[256,128]{0,1:T(8,128)S(1)} %get-tuple-element.63), kind=kOutput, calls=%fused_computation.5 | convolution fusion | flops 202604544 | bytes 4456448 | tf_op jit(solution)/shard_map/while/body/eval_jaxpr/cka,aj->ckj/dot_general | solution.py:46
  60.7 3.1 %convolution_subtract_fusion.1 = f32[8,256,128]{2,1,0:T(8,128)S(1)} fusion(f32[8,256,128]{2,1,0:T(8,128)} %fusion.26, f32[8,256,128]{1,2,0:T(8,128)} %copy-done.1, f32[8,256,128]{1,2,0:T(8,128)} %copy-done.2, f32[256,128]{0,1:T(8,128)S(1)} %get-tuple-element.62, f32[256,128]{0,1:T(8,128)S(1)} %get-tuple-element.63), kind=kOutput, calls=%fused_computation.6 | convolution fusion | flops 202604544 | bytes 4456448 | tf_op jit(solution)/shard_map/while/body/eval_jaxpr/cka,aj->ckj/dot_general | solution.py:43
  63.8 6.4 %all-to-all-done.3 = f32[32,1,512]{2,1,0:T(1,128)S(1)} async-done(((f32[32,1,512]{2,1,0:T(1,128)}), f32[32,1,512]{2,1,0:T(1,128)S(1)}, u32[]{:S(2)}, u32[]{:S(2)}) %all-to-all-start.3) | async-done | bytes 65568 | tf_op jit(solution)/shard_map/all_to_all | solution.py:125
  70.2 1.2 convolution_bitcast_fusion.3
  72.9 1.1 fusion.39
  75.0 1.1 convolution_subtract_fusion.2
  84.2 3.4 %copy.69 = bf16[16384,8]{1,0:T(8,128)(2,1)} copy(bf16[16384,8]{0,1:T(8,128)(2,1)S(1)} %reduce) | data formatting | bytes 524288
  87.6 5.8 %reshape.366 = bf16[16,2,4096]{2,1,0:T(2,128)(2,1)S(1)} reshape(bf16[16384,8]{1,0:T(8,128)(2,1)} %copy.69) | data formatting | bytes 524288
  93.4 13.8 %all_to_all.51 = bf16[16,2,4096]{2,1,0:T(2,128)(2,1)S(1)} all-to-all(bf16[16,2,4096]{2,1,0:T(2,128)(2,1)S(1)} %reshape.366), channel_id=1, replica_groups=mesh['ctx'=16,'chan'=32] {'ctx'}, dimensions={0} | all-to-all | bytes 524288 | tf_op jit(solution)/shard_map/all_to_all | solution.py:168
  107.1 12.3 %reshape.367 = bf16[16384,1,8]{2,1,0:T(2,128)(2,1)} reshape(bf16[16,2,4096]{2,1,0:T(2,128)(2,1)S(1)} %all_to_all.51) | data formatting | bytes 524288
  119.4 14.8 %copy.46 = bf16[16384,1,8]{0,2,1:T(8,128)(2,1)S(1)} copy(bf16[16384,1,8]{2,1,0:T(2,128)(2,1)} %reshape.367) | data formatting | bytes 524288 | tf_op jit(solution)/shard_map/all_to_all | solution.py:168
  (42 shorter events, 18.2 us)
Async XLA Ops:
  0.0 16.4 %copy-start = (f32[256,512]{1,0:T(8,128)S(1)}, f32[256,512]{1,0:T(8,128)}, u32[]{:S(2)}) copy-start(f32[256,512]{1,0:T(8,128)} %param.10) | copy-start | bytes 1572868
  1.9 17.4 %all-to-all-start.1 = ((bf16[1024,16,8]{0,2,1:T(8,128)(2,1)}), bf16[1024,16,8]{0,2,1:T(8,128)(2,1)S(1)}, u32[]{:S(2)}, u32[]{:S(2)}) async-start(bf16[1024,16,8]{0,2,1:T(8,128)(2,1)} %bitcast.16), calls=%async_computation.1 | async-start | bytes 524288 | tf_op jit(solution)/shard_map/all_to_all | solution.py:141
  13.0 29.0 %copy-start.3 = (f32[256,256]{1,0:T(8,128)}, f32[256,256]{1,0:T(8,128)S(1)}, u32[]{:S(2)}) copy-start(f32[256,256]{1,0:T(8,128)S(1)} %fusion.48) | copy-start | bytes 786436
  19.3 11.4 %all-to-all-start.2 = ((bf16[1024,16,8]{0,2,1:T(8,128)(2,1)}), bf16[1024,16,8]{0,2,1:T(8,128)(2,1)S(1)}, u32[]{:S(2)}, u32[]{:S(2)}) async-start(bf16[1024,16,8]{0,2,1:T(8,128)(2,1)} %bitcast.31), calls=%async_computation.2 | async-start | bytes 524288 | tf_op jit(solution)/shard_map/all_to_all | solution.py:148
  30.7 11.4 %all-to-all-start = ((bf16[1024,16,8]{0,2,1:T(8,128)(2,1)}), bf16[1024,16,8]{0,2,1:T(8,128)(2,1)S(1)}, u32[]{:S(2)}, u32[]{:S(2)}) async-start(bf16[1024,16,8]{0,2,1:T(8,128)(2,1)} %bitcast.1), calls=%async_computation | async-start | bytes 524288 | tf_op jit(solution)/shard_map/all_to_all | solution.py:134
  37.1 20.9 %copy-start.1 = (f32[8,256,128]{1,2,0:T(8,128)}, f32[8,256,128]{1,2,0:T(8,128)S(1)}, u32[]{:S(2)}) copy-start(f32[8,256,128]{1,2,0:T(8,128)S(1)} %convolution_bitcast_fusion) | copy-start | bytes 3145732
  37.6 2.2 %copy-start.2 = (f32[8,256,128]{1,2,0:T(8,128)}, f32[8,256,128]{1,2,0:T(8,128)S(1)}, u32[]{:S(2)}) copy-start(f32[8,256,128]{1,2,0:T(8,128)S(1)} %convolution_bitcast_fusion.1) | copy-start | bytes 3145732
  42.1 28.2 %all-to-all-start.3 = ((f32[32,1,512]{2,1,0:T(1,128)}), f32[32,1,512]{2,1,0:T(1,128)S(1)}, u32[]{:S(2)}, u32[]{:S(2)}) async-start(f32[32,1,512]{2,1,0:T(1,128)} %copy.37), calls=%async_computation.3 | async-start | bytes 131072 | tf_op jit(solution)/shard_map/all_to_all | solution.py:125
  75.0 4.8 %copy-start.4 = (f32[256,256]{1,0:T(8,128)S(1)}, f32[256,256]{1,0:T(8,128)}, u32[]{:S(2)}) copy-start(f32[256,256]{1,0:T(8,128)} %copy-done.3) | copy-start | bytes 786436
where the time goes:
time: 136 us; the launch traced here: 135 us
  local copies, waits for them, and re-layouts  46.4 us (34%)
  starting transfers between devices  32.7 us (24%)
  matrix products  22.1 us (16%)
  blocking collectives  13.8 us (10%)
  waiting for transfers between devices  11.7 us (9%)
  other arithmetic  8.13 us (6%)
    unnamed x16, local copies, waits for them, and re-layouts  26.9 us
    all_to_all x1, local copies, waits for them, and re-layouts, local(): lax.all_to_all(gated_cols.T.reshape(seq_len, 1, chan_x), 'ctx', split_axi...  14.8 us
    all_to_all x1, starting transfers between devices, local(): lax.all_to_all(picked, 'chan', split_axis=0, concat_axis=2, tiled=True)  14.3 us
    all_to_all x1, blocking collectives, local(): lax.all_to_all(gated_cols.T.reshape(seq_len, 1, chan_x), 'ctx', split_axi...  13.8 us
    all_to_all x1, starting transfers between devices, local(): lax.all_to_all(key_stream.reshape(pos_rows, ctx_size, chan_x), 'ctx', spl...  10.2 us
    all_to_all x1, waiting for transfers between devices, local(): lax.all_to_all(picked, 'chan', split_axis=0, concat_axis=2, tiled=True)  6.44 us
    all_to_all x1, starting transfers between devices, local(): lax.all_to_all(value_stream.reshape(pos_rows, ctx_size, chan_x), 'ctx', s...  4.14 us
    all_to_all x1, starting transfers between devices, local(): lax.all_to_all(query_stream.reshape(pos_rows, ctx_size, chan_x), 'ctx', s...  4.13 us
  transfers between devices with their start and end apart: 4, of which 4 were waited for; matrix products, arithmetic and copies ran while one was open for 18% of the time, Pallas kernels for 0%

commit v1 on v0

v1 whole, which is shorter than its diff:
```python
import functools

import jax
import jax.numpy as jnp
from jax import lax
from jax.experimental import pallas as pl
from jax.experimental.pallas import tpu as pltpu
from jax.sharding import PartitionSpec as P

GROUP = 16
KSHORT = 7
BLK = 256
LANE = 128
MESH = pl.DeviceIdType.MESH
f32 = jnp.float32
bf16 = jnp.bfloat16


def short_rows(ext, taps, stream, start, count):
    total = taps[stream, 0:1, :] * ext[stream, 16 + start:16 + start + count, :]
    for j in range(1, KSHORT):
        total = total + taps[stream, j:j + 1, :] * ext[stream, 16 + start - j:16 + start - j + count, :]
    return total


def build_toeplitz(taps128, tiles, count):
    row = lax.broadcasted_iota(jnp.int32, (LANE, LANE), 0)
    col = lax.broadcasted_iota(jnp.int32, (LANE, LANE), 1)
    keep = col >= row
    tiles[0] = jnp.zeros((LANE, LANE), bf16)

    def turned(r):
        line = jnp.broadcast_to(taps128[r], (LANE, LANE))
        return pltpu.roll(line, 0, 1, stride=1, stride_axis=0)

    def body(r, before):
        now = turned(r)
        tiles[r + 1] = jnp.where(keep, now, before).astype(bf16)
        return now

    lax.fori_loop(0, count, body, jnp.zeros((LANE, LANE), f32))


def long_conv(xcat, tiles, acc, depth):
    rows = acc.shape[0]
    step = 8 * depth
    for e in range(rows // step):
        parts = []
        for q in range(depth):
            d = e * depth + q
            parts.append(jnp.concatenate([tiles[2 * d + 1], tiles[2 * d + 2]], axis=1))
            parts.append(jnp.concatenate([tiles[2 * d], tiles[2 * d + 1]], axis=1))
        weights = jnp.concatenate(parts, axis=0)
        part = jnp.dot(xcat[0:rows - step * e, :], weights, preferred_element_type=f32)
        if e == 0:
            acc[...] = part
        else:
            acc[step * e:rows, :] += part


DEPTH = 8


def kernel(n_ctx, n_chan, q_hbm, k_hbm, v_hbm, taps_hbm, filt_hbm, skip_hbm, out_hbm,
           raw, taps, filt, skip, ext, halo, qshort, prod, fsend, fgot, xsend, xgot, skipc, xpad, xcat, tiles, acc,
           osend, ogot, outv,
           load_sem, h_send, h_recv, f_send, f_recv, x_send, x_recv, o_send, o_recv):
    me = lax.axis_index("ctx")
    ch = lax.axis_index("chan")
    rows, width = raw.shape[1], raw.shape[2]
    blocks = rows // BLK

    streams = (q_hbm, k_hbm, v_hbm)
    loads = [pltpu.make_async_copy(streams[s], raw.at[s], load_sem.at[s]) for s in range(3)]
    loads.append(pltpu.make_async_copy(taps_hbm, taps, load_sem.at[3]))
    loads.append(pltpu.make_async_copy(skip_hbm, skip, load_sem.at[4]))
    pieces = filt.shape[0]
    for p in range(pieces):
        loads.append(pltpu.make_async_copy(filt_hbm.at[:, LANE * p:LANE * (p + 1)], filt.at[p], load_sem.at[5 + p]))
    for load in loads:
        load.start()

    barrier = pltpu.get_barrier_semaphore()

    def greet_ctx(k, _):
        pl.semaphore_signal(barrier, inc=1, device_id=(lax.rem(me + k, n_ctx), ch), device_id_type=MESH)
        return 0

    def greet_chan(k, _):
        pl.semaphore_signal(barrier, inc=1, device_id=(me, lax.rem(ch + k, n_chan)), device_id_type=MESH)
        return 0

    lax.fori_loop(1, n_chan, greet_chan, 0)
    lax.fori_loop(1, n_ctx, greet_ctx, 0)

    for load in loads:
        load.wait()

    for p in range(pieces):
        fsend[:, p, :] = filt[p, pl.ds(me // 2, n_chan, stride=8), :]

    for s in range(3):
        ext[s, 0:16, :] = jnp.zeros((16, width), f32)
        ext[s, 16:16 + rows, :] = raw[s].astype(f32)
    qshort[...] = short_rows(ext, taps, 0, 0, rows)
    prod[...] = short_rows(ext, taps, 1, 0, rows) * short_rows(ext, taps, 2, 0, rows)
    skipc[...] = jnp.broadcast_to(skip[...], (width, width)).T

    def lay_out(pair):
        both = []
        for i in (2 * pair, 2 * pair + 1):
            both.append(prod[BLK * i:BLK * (i + 1), :].T.reshape(n_ctx, 8, BLK))
        xsend[pair] = jnp.concatenate(both, axis=1).astype(bf16)

    lay_out(1)

    pl.semaphore_wait(barrier, n_ctx - 1 + n_chan - 1)

    @pl.when(me < n_ctx - 1)
    def _():
        for s in range(3):
            pltpu.make_async_remote_copy(raw.at[s, rows - 16:rows], halo.at[s], h_send.at[s], h_recv.at[s],
                                         device_id=(me + 1, ch), device_id_type=MESH).start()

    def filter_copy(to, slot):
        return pltpu.make_async_remote_copy(fsend.at[to], fgot.at[slot], f_send.at[to], f_recv.at[slot],
                                            device_id=(me, to), device_id_type=MESH)

    def send_filter(k, _):
        filter_copy(lax.rem(ch + k, n_chan), ch).start()
        return 0

    lax.fori_loop(1, n_chan, send_filter, 0)
    fgot[ch] = fsend[ch]

    def block_copy(pair, to, slot):
        return pltpu.make_async_remote_copy(xsend.at[pair, to], xgot.at[pair, slot], x_send.at[pair, to],
                                            x_recv.at[pair, slot], device_id=(to, ch), device_id_type=MESH)

    def send_blocks(pair):
        def body(k, _):
            block_copy(pair, lax.rem(me + k, n_ctx), me).start()
            return 0

        lax.fori_loop(1, n_ctx, body, 0)
        xgot[pair, me] = xsend[pair, me]

    send_blocks(1)

    @pl.when(me > 0)
    def _():
        for s in range(3):
            pltpu.make_async_remote_copy(raw.at[s, rows - 16:rows], halo.at[s], h_send.at[s], h_recv.at[s],
                                         device_id=(me - 1, ch), device_id_type=MESH).wait_recv()
            ext[s, 0:16, :] = halo[s].astype(f32)
        qshort[0:8, :] = short_rows(ext, taps, 0, 0, 8)
        prod[0:8, :] = short_rows(ext, taps, 1, 0, 8) * short_rows(ext, taps, 2, 0, 8)

    lay_out(0)
    send_blocks(0)

    def wait_blocks(pair):
        def body(k, _):
            block_copy(pair, lax.rem(me + k, n_ctx), lax.rem(me + k, n_ctx)).wait_recv()
            return 0

        lax.fori_loop(1, n_ctx, body, 0)

    wait_blocks(1)
    wait_blocks(0)

    xpad[0:8 * DEPTH, :] = jnp.zeros((8 * DEPTH, BLK), f32)
    for source in range(n_ctx):
        for pair in range(2):
            start = 8 * DEPTH + 8 * (source * blocks + 2 * pair)
            xpad[start:start + 16, :] = xgot[pair, source].astype(f32)
    total_rows = acc.shape[0]
    for q in range(DEPTH):
        xcat[:, BLK * q:BLK * (q + 1)] = xpad[8 * (DEPTH - q):8 * (DEPTH - q) + total_rows, :].astype(bf16)

    def wait_filter(k, _):
        filter_copy(lax.rem(ch + k, n_chan), lax.rem(ch + k, n_chan)).wait_recv()
        return 0

    lax.fori_loop(1, n_chan, wait_filter, 0)

    class Taps:
        def __getitem__(self, r):
            return fgot[r // 4, pl.ds(lax.rem(r, 4), 1), :]

    build_toeplitz(Taps(), tiles, 4 * n_chan)
    long_conv(xcat, tiles, acc, DEPTH)

    own = skipc[pl.ds(pl.multiple_of(me * 8, 8), 8), :]
    own = jnp.concatenate([own, own], axis=1)
    for dest in range(n_ctx):
        part = acc[dest * 8 * blocks:(dest + 1) * 8 * blocks, :].reshape(blocks, 8, BLK)
        start = 8 * DEPTH + dest * 8 * blocks
        signal = xpad[start:start + 8 * blocks, :].reshape(blocks, 8, BLK)
        osend[dest] = (part + own[None] * signal).astype(bf16).reshape(8 * blocks, BLK)

    def mixed_copy(to, slot):
        return pltpu.make_async_remote_copy(osend.at[to], ogot.at[slot], o_send.at[to], o_recv.at[slot],
                                            device_id=(to, ch), device_id_type=MESH)

    def send_mixed(k, _):
        mixed_copy(lax.rem(me + k, n_ctx), me).start()
        return 0

    lax.fori_loop(1, n_ctx, send_mixed, 0)
    ogot[me] = osend[me]

    def wait_mixed(k, _):
        mixed_copy(lax.rem(me + k, n_ctx), lax.rem(me + k, n_ctx)).wait_recv()
        return 0

    lax.fori_loop(1, n_ctx, wait_mixed, 0)

    wide = ogot[...].astype(f32)
    for i in range(blocks):
        piece = wide[:, 8 * i:8 * (i + 1), :].reshape(width, BLK).T
        rounded = qshort[BLK * i:BLK * (i + 1), :].astype(bf16).astype(f32)
        outv[BLK * i:BLK * (i + 1), :] = (rounded * piece).astype(bf16)
    store = pltpu.make_async_copy(outv, out_hbm, load_sem.at[0])
    store.start()

    @pl.when(me < n_ctx - 1)
    def _():
        for s in range(3):
            pltpu.make_async_remote_copy(raw.at[s, rows - 16:rows], halo.at[s], h_send.at[s], h_recv.at[s],
                                         device_id=(me + 1, ch), device_id_type=MESH).wait_send()

    def end_filter(k, _):
        filter_copy(lax.rem(ch + k, n_chan), ch).wait_send()
        return 0

    lax.fori_loop(1, n_chan, end_filter, 0)

    def end_blocks(k, _):
        to = lax.rem(me + k, n_ctx)
        block_copy(0, to, me).wait_send()
        block_copy(1, to, me).wait_send()
        mixed_copy(to, me).wait_send()
        return 0

    lax.fori_loop(1, n_ctx, end_blocks, 0)
    store.wait()


def local(mesh_shape, query_stream, key_stream, value_stream, short_weight, filter_rows, skip_weight):
    n_ctx, n_chan = mesh_shape
    rows, width = query_stream.shape
    piece = filter_rows.shape[1]
    total = rows * n_ctx // BLK * 8
    dma = pltpu.SemaphoreType.DMA
    return pl.pallas_call(
        functools.partial(kernel, n_ctx, n_chan),
        out_shape=jax.ShapeDtypeStruct((rows, width), bf16),
        in_specs=[pl.BlockSpec(memory_space=pl.ANY)] * 6,
        out_specs=pl.BlockSpec(memory_space=pl.ANY),
        scratch_shapes=[
            pltpu.VMEM((3, rows, width), bf16),
            pltpu.VMEM(short_weight.shape, f32),
            pltpu.VMEM((piece // LANE, filter_rows.shape[0], LANE), f32),
            pltpu.VMEM((1, width), f32),
            pltpu.VMEM((3, rows + 16, width), f32),
            pltpu.VMEM((3, 16, width), bf16),
            pltpu.VMEM((rows, width), f32),
            pltpu.VMEM((rows, width), f32),
            pltpu.VMEM((n_chan, piece // LANE, LANE), f32),
            pltpu.VMEM((n_chan, piece // LANE, LANE), f32),
            pltpu.VMEM((2, n_ctx, 16, BLK), bf16),
            pltpu.VMEM((2, n_ctx, 16, BLK), bf16),
            pltpu.VMEM((width, width), f32),
            pltpu.VMEM((total + 8 * DEPTH, BLK), f32),
            pltpu.VMEM((total, DEPTH * BLK), bf16),
            pltpu.VMEM((n_chan * piece // LANE + 1, LANE, LANE), bf16),
            pltpu.VMEM((total, BLK), f32),
            pltpu.VMEM((n_ctx, total // n_ctx, BLK), bf16),
            pltpu.VMEM((n_ctx, total // n_ctx, BLK), bf16),
            pltpu.VMEM((rows, width), bf16),
            dma((5 + piece // LANE,)),
            dma((3,)), dma((3,)),
            dma((n_chan,)), dma((n_chan,)),
            dma((2, n_ctx)), dma((2, n_ctx)),
            dma((n_ctx,)), dma((n_ctx,)),
        ],
        compiler_params=pltpu.CompilerParams(collective_id=0, has_side_effects=True, vmem_limit_bytes=48 * 1024 * 1024),
    )(query_stream, key_stream, value_stream, short_weight, filter_rows, skip_weight.reshape(1, width))


def solution(mesh):
    return jax.shard_map(
        functools.partial(local, (mesh.shape["ctx"], mesh.shape["chan"])),
        mesh=mesh,
        in_specs=(
            P("ctx", "chan"),
            P("ctx", "chan"),
            P("ctx", "chan"),
            P(None, None, "chan"),
            P(None, "chan"),
            P("chan"),
        ),
        out_specs=P("ctx", "chan"),
        check_vma=False,
    )
```

time: 136 us -> 55.2 us (0.41)
  Pallas kernels: 0 us -> 48.9 us
  local copies, waits for them, and re-layouts: 46.4 us -> 5.96 us
  starting transfers between devices: 32.7 us -> 0 us
  matrix products: 22.1 us -> 0 us
  blocking collectives: 13.8 us -> 0 us
  waiting for transfers between devices: 11.7 us -> 0 us
  other arithmetic: 8.13 us -> 0 us
    pallas_call x0 -> x1, Pallas kernels: none -> 48.9 us  [local(): pl.pallas_call(functools.partial(kernel, n_ctx, n_chan), out_shape=jax.Sh...]
    all_to_all x4 -> x0, starting transfers between devices: 32.7 us -> none  [the longest x1 14.3 us: local(): lax.all_to_all(picked, 'chan', split_axis=0, concat_axis=2, tiled=True)]
    dot_general x18 -> x0, matrix products: 22.1 us -> none  [the longest x2 4.13 us: forward_dft(): jnp.einsum('cka,aj->ckj', turned_im, inner_sin, precision=accuracy)]
    unnamed x16 -> x13, local copies, waits for them, and re-layouts: 26.9 us -> 5.96 us
    all_to_all x1 -> x0, local copies, waits for them, and re-layouts: 14.8 us -> none  [local(): lax.all_to_all(gated_cols.T.reshape(seq_len, 1, chan_x), 'ctx', split_axi...]
    all_to_all x1 -> x0, blocking collectives: 13.8 us -> none  [local(): lax.all_to_all(gated_cols.T.reshape(seq_len, 1, chan_x), 'ctx', split_axi...]
    all_to_all x4 -> x0, waiting for transfers between devices: 11.7 us -> none  [the longest x1 6.44 us: local(): lax.all_to_all(picked, 'chan', split_axis=0, concat_axis=2, tiled=True)]
    convert_element_type x6 -> x0, other arithmetic: 3.73 us -> none  [the longest x1 1.7 us: local(): product = (shorts[1] * shorts[2]).astype(jnp.bfloat16)]
  transfers between devices with their start and end apart: 4 -> 0, of which waited for: 4 -> 0; matrix products, arithmetic and copies ran while one was open for 18% -> 0% of each run, Pallas kernels for 0% -> 0%
where the time goes in v1:
time: 55.2 us; the launch traced here: 54.9 us
  Pallas kernels  48.9 us (89%)
  local copies, waits for them, and re-layouts  5.96 us (11%)
    pallas_call x1, Pallas kernels, local(): pl.pallas_call(functools.partial(kernel, n_ctx, n_chan), out_shape=jax.Sh...  48.9 us
    unnamed x13, local copies, waits for them, and re-layouts  5.96 us

profile of v1, /device:TPU:1, one launch (start us, length us, event | category | flops | bytes accessed | tf_op | source)
XLA Modules:
  0.0 54.9 jit_solution(12453122045576945719)
XLA Ops:
  0.0 0.0 copy-start.5
  0.0 0.7 %copy-done.5 = f32[128]{0:T(128)S(1)} copy-done((f32[128]{0:T(128)S(1)}, f32[128]{0:T(128)}, u32[]{:S(2)}) %copy-start.5) | copy-done | bytes 536
  0.7 0.0 copy-start
  0.7 1.0 %copy-done = f32[256,512]{1,0:T(8,128)S(1)} copy-done((f32[256,512]{1,0:T(8,128)S(1)}, f32[256,512]{1,0:T(8,128)}, u32[]{:S(2)}) %copy-start) | copy-done | bytes 524312
  1.7 0.0 copy-start.1
  1.7 0.9 %copy-done.1 = bf16[1024,128]{1,0:T(8,128)(2,1)S(1)} copy-done((bf16[1024,128]{1,0:T(8,128)(2,1)S(1)}, bf16[1024,128]{1,0:T(8,128)(2,1)}, u32[]{:S(2)}) %copy-start.1) | copy-done | bytes 262168
  2.6 0.0 copy-start.2
  2.7 0.9 %copy-done.2 = bf16[1024,128]{1,0:T(8,128)(2,1)S(1)} copy-done((bf16[1024,128]{1,0:T(8,128)(2,1)S(1)}, bf16[1024,128]{1,0:T(8,128)(2,1)}, u32[]{:S(2)}) %copy-start.2) | copy-done | bytes 262168
  3.6 0.0 copy-start.3
  3.6 0.9 %copy-done.3 = bf16[1024,128]{1,0:T(8,128)(2,1)S(1)} copy-done((bf16[1024,128]{1,0:T(8,128)(2,1)S(1)}, bf16[1024,128]{1,0:T(8,128)(2,1)}, u32[]{:S(2)}) %copy-start.3) | copy-done | bytes 262168
  4.5 0.0 copy-start.4
  4.6 0.7 %copy-done.4 = f32[3,7,128]{2,1,0:T(8,128)S(1)} copy-done((f32[3,7,128]{2,1,0:T(8,128)S(1)}, f32[3,7,128]{2,1,0:T(8,128)}, u32[]{:S(2)}) %copy-start.4) | copy-done | bytes 10776
  5.3 48.9 %shard_map.64 = bf16[1024,128]{1,0:T(8,128)(2,1)S(1)} custom-call(bf16[1024,128]{1,0:T(8,128)(2,1)S(1)} %copy-done.1, bf16[1024,128]{1,0:T(8,128)(2,1)S(1)} %copy-done.2, bf16[1024,128]{1,0:T(8,128)(2,1)S(1)} %copy-done.3, f32[3,7,128]{2,1,0:T(8,128)S(1)} %copy-done.4, f32[256,512]{1,0:T(8,128)S(1)} %copy-done, f32[1,128]{1,0:T(1,128)S(1)} %bitcast.1), custom_call_target="tpu_custom_call" | custom-call | tf_op jit(solution)/shard_map/pallas_call | solution.py:256
  54.2 0.7 %copy.8 = bf16[1024,128]{1,0:T(8,128)(2,1)} copy(bf16[1024,128]{1,0:T(8,128)(2,1)S(1)} %shard_map.64) | data formatting | bytes 524288
Async XLA Ops:
  0.0 0.7 %copy-start.5 = (f32[128]{0:T(128)S(1)}, f32[128]{0:T(128)}, u32[]{:S(2)}) copy-start(f32[128]{0:T(128)} %param.11) | copy-start | bytes 1540
  0.7 1.0 %copy-start = (f32[256,512]{1,0:T(8,128)S(1)}, f32[256,512]{1,0:T(8,128)}, u32[]{:S(2)}) copy-start(f32[256,512]{1,0:T(8,128)} %filt_hbm.1) | copy-start | bytes 1572868
  1.7 0.9 %copy-start.1 = (bf16[1024,128]{1,0:T(8,128)(2,1)S(1)}, bf16[1024,128]{1,0:T(8,128)(2,1)}, u32[]{:S(2)}) copy-start(bf16[1024,128]{1,0:T(8,128)(2,1)} %q_hbm.1) | copy-start | bytes 786436
  2.6 0.9 %copy-start.2 = (bf16[1024,128]{1,0:T(8,128)(2,1)S(1)}, bf16[1024,128]{1,0:T(8,128)(2,1)}, u32[]{:S(2)}) copy-start(bf16[1024,128]{1,0:T(8,128)(2,1)} %k_hbm.1) | copy-start | bytes 786436
  3.6 0.9 %copy-start.3 = (bf16[1024,128]{1,0:T(8,128)(2,1)S(1)}, bf16[1024,128]{1,0:T(8,128)(2,1)}, u32[]{:S(2)}) copy-start(bf16[1024,128]{1,0:T(8,128)(2,1)} %v_hbm.1) | copy-start | bytes 786436
  4.5 0.7 %copy-start.4 = (f32[3,7,128]{2,1,0:T(8,128)S(1)}, f32[3,7,128]{2,1,0:T(8,128)}, u32[]{:S(2)}) copy-start(f32[3,7,128]{2,1,0:T(8,128)} %taps_hbm.1) | copy-start | bytes 32260

commit v2 on v1

--- a/solution.py
+++ b/solution.py
@@ -23,48 +23,38 @@
     return total
 
 
-def build_toeplitz(taps128, tiles, count):
+UNIT = 8
+SHIFTS = UNIT // 2 + 1
+
+
+def unit_tiles(lines, tiles):
     row = lax.broadcasted_iota(jnp.int32, (LANE, LANE), 0)
     col = lax.broadcasted_iota(jnp.int32, (LANE, LANE), 1)
     keep = col >= row
-    tiles[0] = jnp.zeros((LANE, LANE), bf16)
-
-    def turned(r):
-        line = jnp.broadcast_to(taps128[r], (LANE, LANE))
-        return pltpu.roll(line, 0, 1, stride=1, stride_axis=0)
-
-    def body(r, before):
-        now = turned(r)
+    zero = jnp.zeros((LANE, LANE), f32)
+    firsts = [pltpu.roll(jnp.broadcast_to(line, (8, LANE)), 0, 1, stride=1, stride_axis=0) for line in lines]
+    before = zero
+    for r in range(UNIT + 1):
+        now = zero
+        if r < UNIT:
+            now = jnp.concatenate([firsts[r]] + [pltpu.roll(firsts[r], 8 * k, 1) for k in range(1, LANE // 8)], axis=0)
         tiles[r + 1] = jnp.where(keep, now, before).astype(bf16)
-        return now
-
-    lax.fori_loop(0, count, body, jnp.zeros((LANE, LANE), f32))
-
-
-def long_conv(xcat, tiles, acc, depth):
-    rows = acc.shape[0]
-    step = 8 * depth
-    for e in range(rows // step):
-        parts = []
-        for q in range(depth):
-            d = e * depth + q
-            parts.append(jnp.concatenate([tiles[2 * d + 1], tiles[2 * d + 2]], axis=1))
-            parts.append(jnp.concatenate([tiles[2 * d], tiles[2 * d + 1]], axis=1))
-        weights = jnp.concatenate(parts, axis=0)
-        part = jnp.dot(xcat[0:rows - step * e, :], weights, preferred_element_type=f32)
-        if e == 0:
-            acc[...] = part
-        else:
-            acc[step * e:rows, :] += part
-
-
-DEPTH = 8
+        before = now
+
+
+def unit_conv(xcat, tiles, acc, start, rows):
+    parts = []
+    for q in range(SHIFTS):
+        parts.append(jnp.concatenate([tiles[2 * q + 1], tiles[2 * q + 2]], axis=1))
+        parts.append(jnp.concatenate([tiles[2 * q], tiles[2 * q + 1]], axis=1))
+    weights = jnp.concatenate(parts, axis=0)
+    acc[pl.ds(start, rows), :] += jnp.dot(xcat[0:rows, :], weights, preferred_element_type=f32)
 
 
 def kernel(n_ctx, n_chan, q_hbm, k_hbm, v_hbm, taps_hbm, filt_hbm, skip_hbm, out_hbm,
            raw, taps, filt, skip, ext, halo, qshort, prod, fsend, fgot, xsend, xgot, skipc, xpad, xcat, tiles, acc,
            osend, ogot, outv,
-           load_sem, h_send, h_recv, f_send, f_recv, x_send, x_recv, o_send, o_recv):
+           load_sem, ready, h_send, h_recv, f_send, f_recv, x_send, x_recv, o_send, o_recv):
     me = lax.axis_index("ctx")
     ch = lax.axis_index("chan")
     rows, width = raw.shape[1], raw.shape[2]
@@ -86,12 +76,12 @@
         pl.semaphore_signal(barrier, inc=1, device_id=(lax.rem(me + k, n_ctx), ch), device_id_type=MESH)
         return 0
 
-    def greet_chan(k, _):
-        pl.semaphore_signal(barrier, inc=1, device_id=(me, lax.rem(ch + k, n_chan)), device_id_type=MESH)
-        return 0
-
-    lax.fori_loop(1, n_chan, greet_chan, 0)
+    def greet_chan(to, _):
+        pl.semaphore_signal(barrier, inc=1, device_id=(me, to), device_id_type=MESH)
+        return 0
+
     lax.fori_loop(1, n_ctx, greet_ctx, 0)
+    lax.fori_loop(ch + 1, n_chan, greet_chan, 0)
 
     for load in loads:
         load.wait()
@@ -114,7 +104,7 @@
 
     lay_out(1)
 
-    pl.semaphore_wait(barrier, n_ctx - 1 + n_chan - 1)
+    pl.semaphore_wait(barrier, n_ctx - 1 + ch)
 
     @pl.when(me < n_ctx - 1)
     def _():
@@ -126,11 +116,13 @@
         return pltpu.make_async_remote_copy(fsend.at[to], fgot.at[slot], f_send.at[to], f_recv.at[slot],
                                             device_id=(me, to), device_id_type=MESH)
 
-    def send_filter(k, _):
-        filter_copy(lax.rem(ch + k, n_chan), ch).start()
-        return 0
-
-    lax.fori_loop(1, n_chan, send_filter, 0)
+    def send_back(k, _):
+        to = ch - k
+        filter_copy(to, ch).start()
+        pl.semaphore_signal(ready.at[ch], inc=1, device_id=(me, to), device_id_type=MESH)
+        return 0
+
+    lax.fori_loop(1, ch + 1, send_back, 0)
     fgot[ch] = fsend[ch]
 
     def block_copy(pair, to, slot):
@@ -169,33 +161,67 @@
     wait_blocks(1)
     wait_blocks(0)
 
-    xpad[0:8 * DEPTH, :] = jnp.zeros((8 * DEPTH, BLK), f32)
+    xpad[0:8 * SHIFTS, :] = jnp.zeros((8 * SHIFTS, BLK), f32)
     for source in range(n_ctx):
         for pair in range(2):
-            start = 8 * DEPTH + 8 * (source * blocks + 2 * pair)
+            start = 8 * SHIFTS + 8 * (source * blocks + 2 * pair)
             xpad[start:start + 16, :] = xgot[pair, source].astype(f32)
-    total_rows = acc.shape[0]
-    for q in range(DEPTH):
-        xcat[:, BLK * q:BLK * (q + 1)] = xpad[8 * (DEPTH - q):8 * (DEPTH - q) + total_rows, :].astype(bf16)
-
-    def wait_filter(k, _):
-        filter_copy(lax.rem(ch + k, n_chan), lax.rem(ch + k, n_chan)).wait_recv()
-        return 0
-
-    lax.fori_loop(1, n_chan, wait_filter, 0)
-
-    class Taps:
-        def __getitem__(self, r):
-            return fgot[r // 4, pl.ds(lax.rem(r, 4), 1), :]
-
-    build_toeplitz(Taps(), tiles, 4 * n_chan)
-    long_conv(xcat, tiles, acc, DEPTH)
+    for q in range(SHIFTS):
+        xcat[:, BLK * q:BLK * (q + 1)] = xpad[8 * (SHIFTS - q):8 * (SHIFTS - q) + xcat.shape[0], :].astype(bf16)
+    acc[...] = jnp.zeros_like(acc)
+
+    n_unit = n_chan // 2
+    mine = ch // 2
+
+    def unit_at(s):
+        low = jnp.where(s > 2 * mine, s, jnp.where(s % 2 == 1, mine + (s + 1) // 2, mine - s // 2))
+        step = jnp.where(s % 2 == 1, n_unit - (s + 1) // 2, s // 2)
+        high = lax.rem(mine + step, n_unit)
+        return jnp.where(mine < n_unit // 2, low, high)
+
+    def forward(unit):
+        for y in range(2):
+            to = 2 * unit + y
+
+            @pl.when(to > ch)
+            def _():
+                pl.semaphore_wait(ready.at[to], 1)
+                filter_copy(to, ch).start()
+
+    def add_unit(s, _):
+        unit = unit_at(s)
+
+        @pl.when(s < n_unit - 1)
+        def _():
+            forward(unit_at(s + 1))
+
+        for y in range(2):
+            source = 2 * unit + y
+
+            @pl.when(source != ch)
+            def _():
+                filter_copy(source, source).wait_recv()
+
+        taps_of = [fgot[2 * unit + r // 4, r % 4:r % 4 + 1, :] for r in range(UNIT)]
+        unit_tiles(taps_of, tiles)
+        span = 8 * UNIT // 2
+        quarter = n_unit // 4
+        for part in range(4):
+            @pl.when(unit // quarter == part)
+            def _():
+                unit_conv(xcat, tiles, acc, pl.multiple_of(span * unit, span), xcat.shape[0] - span * quarter * part)
+        return 0
+
+    tiles[0] = jnp.zeros((LANE, LANE), bf16)
+    tiles[UNIT + 2] = jnp.zeros((LANE, LANE), bf16)
+    forward(mine)
+    lax.fori_loop(0, n_unit, add_unit, 0)
 
     own = skipc[pl.ds(pl.multiple_of(me * 8, 8), 8), :]
     own = jnp.concatenate([own, own], axis=1)
     for dest in range(n_ctx):
         part = acc[dest * 8 * blocks:(dest + 1) * 8 * blocks, :].reshape(blocks, 8, BLK)
-        start = 8 * DEPTH + dest * 8 * blocks
+        start = 8 * SHIFTS + dest * 8 * blocks
         signal = xpad[start:start + 8 * blocks, :].reshape(blocks, 8, BLK)
         osend[dest] = (part + own[None] * signal).astype(bf16).reshape(8 * blocks, BLK)
 
@@ -256,7 +282,7 @@
     return pl.pallas_call(
         functools.partial(kernel, n_ctx, n_chan),
         out_shape=jax.ShapeDtypeStruct((rows, width), bf16),
-        in_specs=[pl.BlockSpec(memory_space=pl.ANY)] * 6,
+        in_specs=[pl.BlockSpec(memory_space=pltpu.HBM)] * 6,
         out_specs=pl.BlockSpec(memory_space=pl.ANY),
         scratch_shapes=[
             pltpu.VMEM((3, rows, width), bf16),
@@ -272,20 +298,21 @@
             pltpu.VMEM((2, n_ctx, 16, BLK), bf16),
             pltpu.VMEM((2, n_ctx, 16, BLK), bf16),
             pltpu.VMEM((width, width), f32),
-            pltpu.VMEM((total + 8 * DEPTH, BLK), f32),
-            pltpu.VMEM((total, DEPTH * BLK), bf16),
-            pltpu.VMEM((n_chan * piece // LANE + 1, LANE, LANE), bf16),
-            pltpu.VMEM((total, BLK), f32),
+            pltpu.VMEM((total + 8 * SHIFTS, BLK), f32),
+            pltpu.VMEM((total, SHIFTS * BLK), bf16),
+            pltpu.VMEM((UNIT + 3, LANE, LANE), bf16),
+            pltpu.VMEM((total + total // 2, BLK), f32),
             pltpu.VMEM((n_ctx, total // n_ctx, BLK), bf16),
             pltpu.VMEM((n_ctx, total // n_ctx, BLK), bf16),
             pltpu.VMEM((rows, width), bf16),
             dma((5 + piece // LANE,)),
+            pltpu.SemaphoreType.REGULAR((n_chan,)),
             dma((3,)), dma((3,)),
             dma((n_chan,)), dma((n_chan,)),
             dma((2, n_ctx)), dma((2, n_ctx)),
             dma((n_ctx,)), dma((n_ctx,)),
         ],
-        compiler_params=pltpu.CompilerParams(collective_id=0, has_side_effects=True, vmem_limit_bytes=48 * 1024 * 1024),
+        compiler_params=pltpu.CompilerParams(collective_id=0, has_side_effects=True, vmem_limit_bytes=63 * 1024 * 1024),
     )(query_stream, key_stream, value_stream, short_weight, filter_rows, skip_weight.reshape(1, width))
 
 

time: 55.2 us -> 49.8 us (0.902)
  the two profiles are of different devices: /device:TPU:1 before, /device:TPU:481 now
where the time goes in v2:
time: 49.8 us; the launch traced here: 49.6 us
  Pallas kernels  47.9 us (96%)
  local copies, waits for them, and re-layouts  1.67 us (3%)
    pallas_call x1, Pallas kernels, local(): pl.pallas_call(functools.partial(kernel, n_ctx, n_chan), out_shape=jax.Sh...  47.9 us
    unnamed x1, local copies, waits for them, and re-layouts  1.67 us

profile of v2, /device:TPU:481, one launch (start us, length us, event | category | flops | bytes accessed | tf_op | source)
XLA Modules:
  0.0 49.6 jit_solution(702588661472127462)
XLA Ops:
  0.0 47.9 %shard_map.64 = bf16[1024,128]{1,0:T(8,128)(2,1)} custom-call(bf16[1024,128]{1,0:T(8,128)(2,1)} %q_hbm.1, bf16[1024,128]{1,0:T(8,128)(2,1)} %k_hbm.1, bf16[1024,128]{1,0:T(8,128)(2,1)} %v_hbm.1, f32[3,7,128]{2,1,0:T(8,128)} %taps_hbm.1, f32[256,512]{1,0:T(8,128)} %filt_hbm.1, f32[1,128]{1,0:T(1,128)} %bitcast.1), custom_call_target="tpu_custom_call" | custom-call | tf_op jit(solution)/shard_map/pallas_call | solution.py:282
  47.9 1.7 %copy.8 = bf16[1024,128]{1,0:T(8,128)(2,1)} copy(bf16[1024,128]{1,0:T(8,128)(2,1)} %shard_map.64) | data formatting | bytes 524288

commit v3 on v2

--- a/solution.py
+++ b/solution.py
@@ -24,35 +24,50 @@
 
 
 UNIT = 8
-SHIFTS = UNIT // 2 + 1
-
-
-def unit_tiles(lines, tiles):
+DEPTH = 8
+
+
+def unit_tiles(lines, tiles, lower, unit):
     row = lax.broadcasted_iota(jnp.int32, (LANE, LANE), 0)
     col = lax.broadcasted_iota(jnp.int32, (LANE, LANE), 1)
     keep = col >= row
     zero = jnp.zeros((LANE, LANE), f32)
     firsts = [pltpu.roll(jnp.broadcast_to(line, (8, LANE)), 0, 1, stride=1, stride_axis=0) for line in lines]
     before = zero
-    for r in range(UNIT + 1):
-        now = zero
-        if r < UNIT:
-            now = jnp.concatenate([firsts[r]] + [pltpu.roll(firsts[r], 8 * k, 1) for k in range(1, LANE // 8)], axis=0)
-        tiles[r + 1] = jnp.where(keep, now, before).astype(bf16)
+    for r in range(UNIT):
+        now = jnp.concatenate([firsts[r]] + [pltpu.roll(firsts[r], 8 * k, 1) for k in range(1, LANE // 8)], axis=0)
+        tiles[UNIT * unit + r + 1] = jnp.where(keep, now, before).astype(bf16)
         before = now
-
-
-def unit_conv(xcat, tiles, acc, start, rows):
-    parts = []
-    for q in range(SHIFTS):
-        parts.append(jnp.concatenate([tiles[2 * q + 1], tiles[2 * q + 2]], axis=1))
-        parts.append(jnp.concatenate([tiles[2 * q], tiles[2 * q + 1]], axis=1))
-    weights = jnp.concatenate(parts, axis=0)
-    acc[pl.ds(start, rows), :] += jnp.dot(xcat[0:rows, :], weights, preferred_element_type=f32)
+    lower[unit] = jnp.where(keep, zero, before).astype(bf16)
+
+
+def join_units(tiles, lower, units):
+    for unit in range(1, units):
+        tiles[UNIT * unit + 1] = tiles[UNIT * unit + 1] + lower[unit - 1]
+    tiles[UNIT * units + 1] = lower[units - 1]
+
+
+def half_conv(xcat, tiles, acc, which, depths):
+    total = xcat.shape[0]
+    first = which * 8 * depths
+    for e in range(depths // DEPTH):
+        parts = []
+        for q in range(DEPTH):
+            d = e * DEPTH + q
+            parts.append(jnp.concatenate([tiles[2 * d + 1], tiles[2 * d + 2]], axis=1))
+            parts.append(jnp.concatenate([tiles[2 * d], tiles[2 * d + 1]], axis=1))
+        start = first + 8 * DEPTH * e
+        acc[start:total, :] += jnp.dot(xcat[0:total - start, :], jnp.concatenate(parts, axis=0), preferred_element_type=f32)
+    start = first + 8 * depths
+    if start < total:
+        d = depths
+        weights = jnp.concatenate([jnp.concatenate([tiles[2 * d + 1], tiles[2 * d + 2]], axis=1),
+                                   jnp.concatenate([tiles[2 * d], tiles[2 * d + 1]], axis=1)], axis=0)
+        acc[start:total, :] += jnp.dot(xcat[0:total - start, 0:BLK], weights, preferred_element_type=f32)
 
 
 def kernel(n_ctx, n_chan, q_hbm, k_hbm, v_hbm, taps_hbm, filt_hbm, skip_hbm, out_hbm,
-           raw, taps, filt, skip, ext, halo, qshort, prod, fsend, fgot, xsend, xgot, skipc, xpad, xcat, tiles, acc,
+           raw, taps, filt, skip, ext, halo, qshort, prod, fsend, fgot, xsend, xgot, skipc, xpad, xcat, tiles, lower, acc,
            osend, ogot, outv,
            load_sem, ready, h_send, h_recv, f_send, f_recv, x_send, x_recv, o_send, o_recv):
     me = lax.axis_index("ctx")
@@ -89,20 +104,16 @@
     for p in range(pieces):
         fsend[:, p, :] = filt[p, pl.ds(me // 2, n_chan, stride=8), :]
 
-    for s in range(3):
-        ext[s, 0:16, :] = jnp.zeros((16, width), f32)
-        ext[s, 16:16 + rows, :] = raw[s].astype(f32)
-    qshort[...] = short_rows(ext, taps, 0, 0, rows)
-    prod[...] = short_rows(ext, taps, 1, 0, rows) * short_rows(ext, taps, 2, 0, rows)
-    skipc[...] = jnp.broadcast_to(skip[...], (width, width)).T
-
     def lay_out(pair):
         both = []
         for i in (2 * pair, 2 * pair + 1):
             both.append(prod[BLK * i:BLK * (i + 1), :].T.reshape(n_ctx, 8, BLK))
         xsend[pair] = jnp.concatenate(both, axis=1).astype(bf16)
 
-    lay_out(1)
+    skipc[...] = jnp.broadcast_to(skip[...], (width, width)).T
+    acc[...] = jnp.zeros_like(acc)
+    tiles[0] = jnp.zeros((LANE, LANE), bf16)
+    tiles[tiles.shape[0] - 1] = jnp.zeros((LANE, LANE), bf16)
 
     pl.semaphore_wait(barrier, n_ctx - 1 + ch)
 
@@ -137,6 +148,11 @@
         lax.fori_loop(1, n_ctx, body, 0)
         xgot[pair, me] = xsend[pair, me]
 
+    for s in range(3):
+        ext[s, 0:16, :] = jnp.zeros((16, width), f32)
+        ext[s, 16:16 + rows, :] = raw[s].astype(f32)
+    prod[...] = short_rows(ext, taps, 1, 0, rows) * short_rows(ext, taps, 2, 0, rows)
+    lay_out(1)
     send_blocks(1)
 
     @pl.when(me > 0)
@@ -145,11 +161,52 @@
             pltpu.make_async_remote_copy(raw.at[s, rows - 16:rows], halo.at[s], h_send.at[s], h_recv.at[s],
                                          device_id=(me - 1, ch), device_id_type=MESH).wait_recv()
             ext[s, 0:16, :] = halo[s].astype(f32)
-        qshort[0:8, :] = short_rows(ext, taps, 0, 0, 8)
         prod[0:8, :] = short_rows(ext, taps, 1, 0, 8) * short_rows(ext, taps, 2, 0, 8)
 
     lay_out(0)
     send_blocks(0)
+    qshort[...] = short_rows(ext, taps, 0, 0, rows)
+
+    n_unit = n_chan // 2
+    half = n_unit // 2
+    mine = ch // 2
+    place = lax.rem(mine, half)
+    base = mine - place
+    early = mine < half
+
+    def unit_at(s):
+        turn = jnp.where(s < half, s, n_unit - 1 - s)
+        swing = jnp.where(turn % 2 == 1, place + (turn + 1) // 2, place - turn // 2)
+        rest = jnp.where(place < half // 2, turn, half - 1 - turn)
+        local_unit = jnp.where(turn <= 2 * jnp.minimum(place, half - 1 - place), swing, rest)
+        return jnp.where(s < half, base, half - base) + local_unit
+
+    def answer(s, _):
+        for y in range(2):
+            to = 2 * unit_at(s) + y
+
+            @pl.when(to > ch)
+            def _():
+                pl.semaphore_wait(ready.at[to], 1)
+                filter_copy(to, ch).start()
+        return 0
+
+    def take_unit(s, _):
+        unit = unit_at(s)
+
+        @pl.when(s + 1 < half)
+        def _():
+            answer(s + 1, 0)
+
+        for y in range(2):
+            source = 2 * unit + y
+
+            @pl.when(source != ch)
+            def _():
+                filter_copy(source, source).wait_recv()
+
+        unit_tiles([fgot[2 * unit + r // 4, r % 4:r % 4 + 1, :] for r in range(UNIT)], tiles, lower, lax.rem(unit, half))
+        return 0
 
     def wait_blocks(pair):
         def body(k, _):
@@ -158,82 +215,81 @@
 
         lax.fori_loop(1, n_ctx, body, 0)
 
-    wait_blocks(1)
-    wait_blocks(0)
-
-    xpad[0:8 * SHIFTS, :] = jnp.zeros((8 * SHIFTS, BLK), f32)
-    for source in range(n_ctx):
-        for pair in range(2):
-            start = 8 * SHIFTS + 8 * (source * blocks + 2 * pair)
-            xpad[start:start + 16, :] = xgot[pair, source].astype(f32)
-    for q in range(SHIFTS):
-        xcat[:, BLK * q:BLK * (q + 1)] = xpad[8 * (SHIFTS - q):8 * (SHIFTS - q) + xcat.shape[0], :].astype(bf16)
-    acc[...] = jnp.zeros_like(acc)
-
-    n_unit = n_chan // 2
-    mine = ch // 2
-
-    def unit_at(s):
-        low = jnp.where(s > 2 * mine, s, jnp.where(s % 2 == 1, mine + (s + 1) // 2, mine - s // 2))
-        step = jnp.where(s % 2 == 1, n_unit - (s + 1) // 2, s // 2)
-        high = lax.rem(mine + step, n_unit)
-        return jnp.where(mine < n_unit // 2, low, high)
-
-    def forward(unit):
-        for y in range(2):
-            to = 2 * unit + y
-
-            @pl.when(to > ch)
-            def _():
-                pl.semaphore_wait(ready.at[to], 1)
-                filter_copy(to, ch).start()
-
-    def add_unit(s, _):
-        unit = unit_at(s)
-
-        @pl.when(s < n_unit - 1)
-        def _():
-            forward(unit_at(s + 1))
-
-        for y in range(2):
-            source = 2 * unit + y
-
-            @pl.when(source != ch)
-            def _():
-                filter_copy(source, source).wait_recv()
-
-        taps_of = [fgot[2 * unit + r // 4, r % 4:r % 4 + 1, :] for r in range(UNIT)]
-        unit_tiles(taps_of, tiles)
-        span = 8 * UNIT // 2
-        quarter = n_unit // 4
-        for part in range(4):
-            @pl.when(unit // quarter == part)
-            def _():
-                unit_conv(xcat, tiles, acc, pl.multiple_of(span * unit, span), xcat.shape[0] - span * quarter * part)
-        return 0
-
-    tiles[0] = jnp.zeros((LANE, LANE), bf16)
-    tiles[UNIT + 2] = jnp.zeros((LANE, LANE), bf16)
-    forward(mine)
-    lax.fori_loop(0, n_unit, add_unit, 0)
-
-    own = skipc[pl.ds(pl.multiple_of(me * 8, 8), 8), :]
-    own = jnp.concatenate([own, own], axis=1)
-    for dest in range(n_ctx):
-        part = acc[dest * 8 * blocks:(dest + 1) * 8 * blocks, :].reshape(blocks, 8, BLK)
-        start = 8 * SHIFTS + dest * 8 * blocks
-        signal = xpad[start:start + 8 * blocks, :].reshape(blocks, 8, BLK)
-        osend[dest] = (part + own[None] * signal).astype(bf16).reshape(8 * blocks, BLK)
-
     def mixed_copy(to, slot):
         return pltpu.make_async_remote_copy(osend.at[to], ogot.at[slot], o_send.at[to], o_recv.at[slot],
                                             device_id=(to, ch), device_id_type=MESH)
 
-    def send_mixed(k, _):
-        mixed_copy(lax.rem(me + k, n_ctx), me).start()
-        return 0
-
-    lax.fori_loop(1, n_ctx, send_mixed, 0)
+    own = skipc[pl.ds(pl.multiple_of(me * 8, 8), 8), :]
+    own = jnp.concatenate([own, own], axis=1)
+
+    def mix(dests):
+        for dest in dests:
+            part = acc[dest * 8 * blocks:(dest + 1) * 8 * blocks, :].reshape(blocks, 8, BLK)
+            start = 8 * DEPTH + dest * 8 * blocks
+            signal = xpad[start:start + 8 * blocks, :].reshape(blocks, 8, BLK)
+            osend[dest] = (part + own[None] * signal).astype(bf16).reshape(8 * blocks, BLK)
+
+    def send_mixed(first, count):
+        def body(k, _):
+            to = first + lax.rem(me + k, count)
+
+            @pl.when(to != me)
+            def _():
+                mixed_copy(to, me).start()
+            return 0
+
+        lax.fori_loop(0, count, body, 0)
+
+    answer(0, 0)
+
+    def phase(p, _):
+        lax.fori_loop(half * p, half * (p + 1), take_unit, 0)
+        join_units(tiles, lower, half)
+
+        @pl.when(p == 0)
+        def _():
+            @pl.when(early)
+            def _():
+                lax.fori_loop(half, n_unit, answer, 0)
+
+            wait_blocks(1)
+            wait_blocks(0)
+            xpad[0:8 * DEPTH, :] = jnp.zeros((8 * DEPTH, BLK), f32)
+            for source in range(n_ctx):
+                for pair in range(2):
+                    start = 8 * DEPTH + 8 * (source * blocks + 2 * pair)
+                    xpad[start:start + 16, :] = xgot[pair, source].astype(f32)
+            for q in range(DEPTH):
+                xcat[:, BLK * q:BLK * (q + 1)] = xpad[8 * (DEPTH - q):8 * (DEPTH - q) + xcat.shape[0], :].astype(bf16)
+
+        lower_half = early == (p == 0)
+
+        @pl.when(lower_half)
+        def _():
+            half_conv(xcat, tiles, acc, 0, half * UNIT // 2)
+
+        @pl.when(jnp.logical_not(lower_half))
+        def _():
+            half_conv(xcat, tiles, acc, 1, half * UNIT // 2)
+
+        @pl.when(jnp.logical_and(early, p == 0))
+        def _():
+            mix(range(n_ctx // 2))
+            send_mixed(0, n_ctx // 2)
+        return 0
+
+    lax.fori_loop(0, 2, phase, 0)
+
+    @pl.when(early)
+    def _():
+        mix(range(n_ctx // 2, n_ctx))
+        send_mixed(n_ctx // 2, n_ctx // 2)
+
+    @pl.when(jnp.logical_not(early))
+    def _():
+        mix(range(n_ctx))
+        send_mixed(0, n_ctx)
+
     ogot[me] = osend[me]
 
     def wait_mixed(k, _):
@@ -298,10 +354,11 @@
             pltpu.VMEM((2, n_ctx, 16, BLK), bf16),
             pltpu.VMEM((2, n_ctx, 16, BLK), bf16),
             pltpu.VMEM((width, width), f32),
-            pltpu.VMEM((total + 8 * SHIFTS, BLK), f32),
-            pltpu.VMEM((total, SHIFTS * BLK), bf16),
-            pltpu.VMEM((UNIT + 3, LANE, LANE), bf16),
-            pltpu.VMEM((total + total // 2, BLK), f32),
+            pltpu.VMEM((total + 8 * DEPTH, BLK), f32),
+            pltpu.VMEM((total, DEPTH * BLK), bf16),
+            pltpu.VMEM((n_chan // 4 * UNIT + 3, LANE, LANE), bf16),
+            pltpu.VMEM((n_chan // 4, LANE, LANE), bf16),
+            pltpu.VMEM((total, BLK), f32),
             pltpu.VMEM((n_ctx, total // n_ctx, BLK), bf16),
             pltpu.VMEM((n_ctx, total // n_ctx, BLK), bf16),
             pltpu.VMEM((rows, width), bf16),

time: 49.8 us -> 38.9 us (0.78)
  Pallas kernels: 47.9 us -> 37 us
    pallas_call x1, Pallas kernels: 47.9 us -> 37 us  [local(): pl.pallas_call(functools.partial(kernel, n_ctx, n_chan), out_shape=jax.Sh...]
where the time goes in v3:
time: 38.9 us; the launch traced here: 38.7 us
  Pallas kernels  37 us (95%)
  local copies, waits for them, and re-layouts  1.67 us (4%)
    pallas_call x1, Pallas kernels, local(): pl.pallas_call(functools.partial(kernel, n_ctx, n_chan), out_shape=jax.Sh...  37 us
    unnamed x1, local copies, waits for them, and re-layouts  1.67 us

profile of v3, /device:TPU:481, one launch (start us, length us, event | category | flops | bytes accessed | tf_op | source)
XLA Modules:
  0.0 38.7 jit_solution(7493142196029964614)
XLA Ops:
  0.0 37.0 %shard_map.64 = bf16[1024,128]{1,0:T(8,128)(2,1)} custom-call(bf16[1024,128]{1,0:T(8,128)(2,1)} %q_hbm.1, bf16[1024,128]{1,0:T(8,128)(2,1)} %k_hbm.1, bf16[1024,128]{1,0:T(8,128)(2,1)} %v_hbm.1, f32[3,7,128]{2,1,0:T(8,128)} %taps_hbm.1, f32[256,512]{1,0:T(8,128)} %filt_hbm.1, f32[1,128]{1,0:T(1,128)} %bitcast.1), custom_call_target="tpu_custom_call" | custom-call | tf_op jit(solution)/shard_map/pallas_call | solution.py:338
  37.0 1.7 %copy.8 = bf16[1024,128]{1,0:T(8,128)(2,1)} copy(bf16[1024,128]{1,0:T(8,128)(2,1)} %shard_map.64) | data formatting | bytes 524288

commit v4 on v3

--- a/solution.py
+++ b/solution.py
@@ -87,16 +87,28 @@
 
     barrier = pltpu.get_barrier_semaphore()
 
+    core = lax.rem(me, 2)
+    first = me - core
+
     def greet_ctx(k, _):
-        pl.semaphore_signal(barrier, inc=1, device_id=(lax.rem(me + k, n_ctx), ch), device_id_type=MESH)
-        return 0
-
-    def greet_chan(to, _):
-        pl.semaphore_signal(barrier, inc=1, device_id=(me, to), device_id_type=MESH)
-        return 0
-
+        to = lax.rem(me + k, n_ctx)
+
+        @pl.when(lax.rem(to, 2) == 0)
+        def _():
+            pl.semaphore_signal(barrier, inc=1, device_id=(to, ch), device_id_type=MESH)
+        return 0
+
+    def greet_after(to, _):
+        pl.semaphore_signal(barrier, inc=1, device_id=(first, to), device_id_type=MESH)
+        return 0
+
+    def greet_before(to, _):
+        pl.semaphore_signal(barrier, inc=1, device_id=(first + 1, to), device_id_type=MESH)
+        return 0
+
+    lax.fori_loop(0, ch, greet_before, 0)
+    lax.fori_loop(ch + 1, n_chan, greet_after, 0)
     lax.fori_loop(1, n_ctx, greet_ctx, 0)
-    lax.fori_loop(ch + 1, n_chan, greet_chan, 0)
 
     for load in loads:
         load.wait()
@@ -115,26 +127,38 @@
     tiles[0] = jnp.zeros((LANE, LANE), bf16)
     tiles[tiles.shape[0] - 1] = jnp.zeros((LANE, LANE), bf16)
 
-    pl.semaphore_wait(barrier, n_ctx - 1 + ch)
+    def filter_copy(to, side):
+        return pltpu.make_async_remote_copy(fsend.at[to], fgot.at[ch], f_send.at[side, to], f_recv.at[ch],
+                                            device_id=(first + side, to), device_id_type=MESH)
+
+    def send_filter(to, _):
+        for side in range(2):
+            filter_copy(to, side).start()
+        return 0
+
+    @pl.when(core == 0)
+    def _():
+        pl.semaphore_wait(barrier, n_ctx - 1 + 2 * ch)
+        pl.semaphore_signal(ready, inc=1, device_id=(me + 1, ch), device_id_type=MESH)
+        lax.fori_loop(0, ch, send_filter, 0)
+
+    @pl.when(core == 1)
+    def _():
+        pl.semaphore_wait(ready, 1)
+
+    def send_after():
+        @pl.when(ch < n_chan - 1)
+        def _():
+            pl.semaphore_wait(barrier, 2 * (n_chan - 1 - ch))
+            lax.fori_loop(ch + 1, n_chan, send_filter, 0)
+
+    fgot[ch] = fsend[ch]
 
     @pl.when(me < n_ctx - 1)
     def _():
         for s in range(3):
             pltpu.make_async_remote_copy(raw.at[s, rows - 16:rows], halo.at[s], h_send.at[s], h_recv.at[s],
                                          device_id=(me + 1, ch), device_id_type=MESH).start()
-
-    def filter_copy(to, slot):
-        return pltpu.make_async_remote_copy(fsend.at[to], fgot.at[slot], f_send.at[to], f_recv.at[slot],
-                                            device_id=(me, to), device_id_type=MESH)
-
-    def send_back(k, _):
-        to = ch - k
-        filter_copy(to, ch).start()
-        pl.semaphore_signal(ready.at[ch], inc=1, device_id=(me, to), device_id_type=MESH)
-        return 0
-
-    lax.fori_loop(1, ch + 1, send_back, 0)
-    fgot[ch] = fsend[ch]
 
     def block_copy(pair, to, slot):
         return pltpu.make_async_remote_copy(xsend.at[pair, to], xgot.at[pair, slot], x_send.at[pair, to],
@@ -181,32 +205,25 @@
         local_unit = jnp.where(turn <= 2 * jnp.minimum(place, half - 1 - place), swing, rest)
         return jnp.where(s < half, base, half - base) + local_unit
 
-    def answer(s, _):
-        for y in range(2):
-            to = 2 * unit_at(s) + y
-
-            @pl.when(to > ch)
-            def _():
-                pl.semaphore_wait(ready.at[to], 1)
-                filter_copy(to, ch).start()
-        return 0
-
-    def take_unit(s, _):
-        unit = unit_at(s)
-
-        @pl.when(s + 1 < half)
-        def _():
-            answer(s + 1, 0)
-
-        for y in range(2):
-            source = 2 * unit + y
-
-            @pl.when(source != ch)
-            def _():
-                filter_copy(source, source).wait_recv()
-
-        unit_tiles([fgot[2 * unit + r // 4, r % 4:r % 4 + 1, :] for r in range(UNIT)], tiles, lower, lax.rem(unit, half))
-        return 0
+    def take_units(t, _):
+        units = (unit_at(2 * t), unit_at(2 * t + 1))
+        for unit in units:
+            for y in range(2):
+                source = 2 * unit + y
+
+                @pl.when(source != ch)
+                def _():
+                    pltpu.make_async_remote_copy(fsend.at[0], fgot.at[source], f_send.at[0, 0], f_recv.at[source],
+                                                 device_id=(me, source), device_id_type=MESH).wait_recv()
+
+        lines = [[fgot[2 * unit + r // 4, r % 4:r % 4 + 1, :] for r in range(UNIT)] for unit in units]
+        for unit, these in zip(units, lines):
+            unit_tiles(these, tiles, lower, lax.rem(unit, half))
+        return 0
+
+    @pl.when(core == 1)
+    def _():
+        send_after()
 
     def wait_blocks(pair):
         def body(k, _):
@@ -240,18 +257,12 @@
 
         lax.fori_loop(0, count, body, 0)
 
-    answer(0, 0)
-
     def phase(p, _):
-        lax.fori_loop(half * p, half * (p + 1), take_unit, 0)
+        lax.fori_loop(half // 2 * p, half // 2 * (p + 1), take_units, 0)
         join_units(tiles, lower, half)
 
         @pl.when(p == 0)
         def _():
-            @pl.when(early)
-            def _():
-                lax.fori_loop(half, n_unit, answer, 0)
-
             wait_blocks(1)
             wait_blocks(0)
             xpad[0:8 * DEPTH, :] = jnp.zeros((8 * DEPTH, BLK), f32)
@@ -312,11 +323,12 @@
             pltpu.make_async_remote_copy(raw.at[s, rows - 16:rows], halo.at[s], h_send.at[s], h_recv.at[s],
                                          device_id=(me + 1, ch), device_id_type=MESH).wait_send()
 
-    def end_filter(k, _):
-        filter_copy(lax.rem(ch + k, n_chan), ch).wait_send()
-        return 0
-
-    lax.fori_loop(1, n_chan, end_filter, 0)
+    def end_filter(to, _):
+        for side in range(2):
+            filter_copy(to, side).wait_send()
+        return 0
+
+    lax.fori_loop(jnp.where(core == 0, 0, ch + 1), jnp.where(core == 0, ch, n_chan), end_filter, 0)
 
     def end_blocks(k, _):
         to = lax.rem(me + k, n_ctx)
@@ -363,9 +375,9 @@
             pltpu.VMEM((n_ctx, total // n_ctx, BLK), bf16),
             pltpu.VMEM((rows, width), bf16),
             dma((5 + piece // LANE,)),
-            pltpu.SemaphoreType.REGULAR((n_chan,)),
+            pltpu.SemaphoreType.REGULAR,
             dma((3,)), dma((3,)),
-            dma((n_chan,)), dma((n_chan,)),
+            dma((2, n_chan)), dma((n_chan,)),
             dma((2, n_ctx)), dma((2, n_ctx)),
             dma((n_ctx,)), dma((n_ctx,)),
         ],

time: 38.9 us -> 34.8 us (0.89)
  the two profiles are of different devices: /device:TPU:481 before, /device:TPU:25 now
where the time goes in v4:
time: 34.8 us; the launch traced here: 34.6 us
  Pallas kernels  33 us (95%)
  local copies, waits for them, and re-layouts  1.67 us (5%)
    pallas_call x1, Pallas kernels, local(): pl.pallas_call(functools.partial(kernel, n_ctx, n_chan), out_shape=jax.Sh...  33 us
    unnamed x1, local copies, waits for them, and re-layouts  1.67 us

profile of v4, /device:TPU:25, one launch (start us, length us, event | category | flops | bytes accessed | tf_op | source)
XLA Modules:
  0.0 34.6 jit_solution(15723429522124607427)
XLA Ops:
  0.0 33.0 %shard_map.64 = bf16[1024,128]{1,0:T(8,128)(2,1)} custom-call(bf16[1024,128]{1,0:T(8,128)(2,1)} %q_hbm.1, bf16[1024,128]{1,0:T(8,128)(2,1)} %k_hbm.1, bf16[1024,128]{1,0:T(8,128)(2,1)} %v_hbm.1, f32[3,7,128]{2,1,0:T(8,128)} %taps_hbm.1, f32[256,512]{1,0:T(8,128)} %filt_hbm.1, f32[1,128]{1,0:T(1,128)} %bitcast.1), custom_call_target="tpu_custom_call" | custom-call | tf_op jit(solution)/shard_map/pallas_call | solution.py:350
  33.0 1.7 %copy.8 = bf16[1024,128]{1,0:T(8,128)(2,1)} copy(bf16[1024,128]{1,0:T(8,128)(2,1)} %shard_map.64) | data formatting | bytes 524288
